TPU v7x, 32 devices: a whole 2x2x4 slice. The times are simulated.
32 devices in a mesh: tok: 4 (over y, x), hid: 8 (over z, core).
Axes of the slice: x: 2, y: 2, z: 4, core: 2. Of those that a mesh axis runs over, the one named last changes fastest.
Arguments:
- tokens: bfloat16 [6144, 6144], P('tok', 'hid'), may hold values from -6 to 6
- cotangent: bfloat16 [6144, 6144], P('tok', 'hid'), may hold values from -6 to 6
- expert_choice: int32 [6144, 2], P('tok'), may hold values from 0 to 7, as said below
- router: bfloat16 [8, 6144], replicated, may hold values from -0.078125 to 0.078125
- gate_up: bfloat16 [6144, 2, 8192], P('tok', None, 'hid'), may hold values from -0.109375 to 0.109375
- w_down: bfloat16 [6144, 8192], P('tok', 'hid'), may hold values from -0.0625 to 0.0625
Outputs:
- grad_tokens: bfloat16 [6144, 6144], P('tok', 'hid')
- d_combine: float32 [6144, 2], P('tok')
- d_gate_up: float32 [6144, 2, 8192], P('tok', None, 'hid')
- d_down: float32 [6144, 8192], P('tok', 'hid')
Inputs may be any that keep to these rules, and one draw needn't show every extreme that they name: `expert_choice`: each row names 2 different experts. In every aligned block of 1536 rows at most 432 rows name expert 0 and at least half of 432 do; some block has exactly 432.
All inputs are finite; a program needn't handle non-finite values.
Results may differ from a plain program's by a relative error of at most 0.017.
Values may be sent and summed in bfloat16 or wider, within the bound.
A program may use at most 128 MiB of HBM per device.

v0:
```python
import jax
import jax.numpy as jnp
from jax import lax
from jax.sharding import PartitionSpec as P

CAP = 432


def silu_pair(pre):
    sigma = jax.nn.sigmoid(pre)
    return (pre * sigma, sigma * (1.0 + pre * (1.0 - sigma)))


def contract_rows(left, right):
    return lax.dot_general(
        left, right, (((0,), (0,)), ((), ())), preferred_element_type=jnp.float32
    )


def contract_cols(left, right):
    return lax.dot_general(
        left, right, (((1,), (1,)), ((), ())), preferred_element_type=jnp.float32
    )


def local_grads(joined, raw, slot_gate):
    width = raw.shape[1]
    gate_pre = joined[:, :width]
    up_pre = joined[:, width:]
    active, slope = silu_pair(gate_pre)
    product = active * up_pre
    scale = slot_gate[:, None]
    scaled = (scale * product).astype(jnp.bfloat16)
    score_part = jnp.sum(product * raw, axis=1)
    upstream = scale * raw
    grads_mid = jnp.concatenate(
        [
            (upstream * up_pre * slope).astype(jnp.bfloat16),
            (upstream * active).astype(jnp.bfloat16),
        ],
        axis=1,
    )
    return (grads_mid, scaled, score_part)


def local(tokens, cotangent, expert_choice, router, gate_up, w_down):
    local_cols = tokens.shape[1]
    weight_rows = w_down.shape[0]
    hidden_local = w_down.shape[1]
    first = expert_choice[:, 0]
    second = expert_choice[:, 1]
    in_first = first == 0
    in_second = second == 0
    routed = jnp.logical_or(in_first, in_second)
    flags = routed.astype(jnp.int32)
    slot_rank = jnp.cumsum(flags) - flags
    slot_ids = jnp.arange(CAP, dtype=jnp.int32)
    placed = jnp.logical_and(routed[None, :], slot_rank[None, :] == slot_ids[:, None])
    stacked = jnp.concatenate([tokens, cotangent], axis=1)
    dispatched = jnp.dot(
        placed.astype(jnp.bfloat16), stacked, preferred_element_type=jnp.float32
    ).astype(jnp.bfloat16)
    expert_in, expert_cot = (
        lax.all_gather(dispatched[:, :local_cols], "hid", axis=1, tiled=True),
        lax.all_gather(dispatched[:, local_cols:], "hid", axis=1, tiled=True),
    )
    router_cols = lax.dynamic_slice_in_dim(
        router, lax.axis_index("hid") * local_cols, local_cols, 1
    )
    logits = lax.psum(contract_cols(tokens, router_cols), "hid")
    other = first + second
    labels = jnp.arange(logits.shape[1], dtype=jnp.int32)
    other_logit = jnp.sum(jnp.where(other[:, None] == labels[None, :], logits, 0.0), axis=1)
    gating = jnp.where(routed, jax.nn.sigmoid(logits[:, 0] - other_logit), 0.0)
    slot_gate = jnp.sum(jnp.where(placed, gating[None, :], 0.0), axis=1)
    weights_in = gate_up.reshape(weight_rows, 2 * hidden_local)
    spread_in, spread_cot = (
        lax.all_to_all(expert_in, "tok", split_axis=1, concat_axis=0, tiled=True),
        lax.all_to_all(expert_cot, "tok", split_axis=1, concat_axis=0, tiled=True),
    )
    rows_in = spread_in
    rows_cot = spread_cot
    sums = lax.psum_scatter(
        jnp.concatenate(
            [
                jnp.dot(rows_in, weights_in, preferred_element_type=jnp.float32),
                jnp.dot(rows_cot, w_down, preferred_element_type=jnp.float32),
            ],
            axis=1,
        ),
        "tok",
        scatter_dimension=0,
        tiled=True,
    )
    grads_mid, scaled, score_part = local_grads(
        sums[:, : 2 * hidden_local], sums[:, 2 * hidden_local :], slot_gate
    )
    packed = jnp.concatenate([grads_mid, scaled], axis=1)
    piece = lax.all_gather(packed, "tok", axis=0, tiled=True)
    start = jnp.int32(0)
    grad_sum = jnp.zeros((weight_rows, 3 * hidden_local), jnp.float32)
    for group in range(piece.shape[0] // CAP):
        first_row = start + group * CAP
        rows_in = lax.dynamic_slice_in_dim(spread_in, first_row, CAP, 0)
        rows_cot = lax.dynamic_slice_in_dim(spread_cot, first_row, CAP, 0)
        section = piece[group * CAP : (group + 1) * CAP]
        term = jnp.concatenate(
            [
                contract_rows(rows_in, section[:, : 2 * hidden_local]),
                contract_rows(rows_cot, section[:, 2 * hidden_local :]),
            ],
            axis=1,
        )
        grad_sum = grad_sum + lax.optimization_barrier(term.astype(jnp.bfloat16)).astype(
            jnp.float32
        )
    block = contract_cols(piece[:, : 2 * hidden_local], weights_in)
    expert_back = lax.all_to_all(block, "tok", split_axis=0, concat_axis=1, tiled=True)
    back_cols = lax.psum_scatter(expert_back, "hid", scatter_dimension=1, tiled=True)
    scores = lax.psum(score_part, "hid")
    safe = jnp.minimum(slot_rank, CAP - 1)
    grad_tokens = jnp.where(routed[:, None], jnp.take(back_cols, safe, axis=0), 0.0).astype(
        jnp.bfloat16
    )
    token_score = jnp.where(routed, jnp.take(scores, safe, axis=0), 0.0)
    d_combine = jnp.stack(
        [jnp.where(in_first, token_score, 0.0), jnp.where(in_second, token_score, 0.0)], axis=1
    )
    d_gate_up = grad_sum[:, : 2 * hidden_local].reshape(weight_rows, 2, hidden_local)
    d_down = grad_sum[:, 2 * hidden_local :]
    return (grad_tokens, d_combine, d_gate_up, d_down)


def solution(mesh):
    in_specs = (
        P("tok", "hid"),
        P("tok", "hid"),
        P("tok", None),
        P(),
        P("tok", None, "hid"),
        P("tok", "hid"),
    )
    out_specs = (P("tok", "hid"), P("tok", None), P("tok", None, "hid"), P("tok", "hid"))
    return jax.shard_map(local, mesh=mesh, in_specs=in_specs, out_specs=out_specs, check_vma=False)
```

profile of v0, /device:TPU:0, one launch (start us, length us, event | category | flops | bytes accessed | tf_op | source)
XLA Modules:
  0.0 836.1 jit_solution(18197287051668682821)
XLA Ops:
  9.5 4.6 fusion.4
  16.0 58.6 %all-gather.6.cloned.1.call-done = bf16[432,6144]{1,0:T(8,128)(2,1)} async-done(((bf16[432,768]{1,0:T(8,128)(2,1)}), bf16[432,6144]{1,0:T(8,128)(2,1)}) %all-gather.6.cloned.1.call-update) | async-done | bytes 5308432 | tf_op jit(solution)/shard_map/all_gather | solution.py:65
  74.6 5.3 copy.41
  80.0 5.2 all-to-all-start.1
  85.2 47.0 %all-gather.4.cloned.1.call-done = bf16[432,6144]{1,0:T(8,128)(2,1)} async-done(((bf16[432,768]{1,0:T(8,128)(2,1)}), bf16[432,6144]{1,0:T(8,128)(2,1)}) %all-gather.4.cloned.1.call-update) | async-done | bytes 5308432 | tf_op jit(solution)/shard_map/all_gather | solution.py:64
  132.1 5.4 copy.42
  137.5 7.7 all-to-all-done.1
  145.2 5.0 all-to-all-start
  150.8 8.1 copy.36
  158.9 10.2 %fusion.27 = f32[1728,1024]{1,0:T(8,128)} fusion(bf16[1728,1536]{1,0:T(8,128)(2,1)} %bitcast.5, bf16[1536,1024]{1,0:T(8,128)(2,1)S(1)} %copy-done), kind=kOutput, calls=%fused_computation.80 | convolution fusion | flops 5435817984 | bytes 15532032 | tf_op jit(solution)/shard_map/dot_general | solution.py:87
  169.1 40.3 %all-to-all-done = bf16[432,4,1536]{2,0,1:T(8,128)(2,1)} async-done(((bf16[432,4,1536]{2,0,1:T(8,128)(2,1)}), bf16[432,4,1536]{2,0,1:T(8,128)(2,1)}, u32[]{:S(2)}, u32[]{:S(2)}) %all-to-all-start) | async-done | bytes 5308448 | tf_op jit(solution)/shard_map/all_to_all | solution.py:78
  209.4 15.1 %fusion.26 = f32[1728,2048]{1,0:T(8,128)S(1)} fusion(bf16[1728,1536]{1,0:T(8,128)(2,1)} %bitcast.3, bf16[1536,2048]{1,0:T(8,128)(2,1)} %bitcast.75), kind=kOutput, calls=%fused_computation.79 | convolution fusion | flops 10871635968 | bytes 25755648 | tf_op jit(solution)/shard_map/dot_general | solution.py:86
  224.5 7.4 pad_maximum_fusion
  235.0 184.7 %reduce-scatter.3.cloned.1.call-done = f32[432,3072]{1,0:T(8,128)} async-done(((f32[1728,3072]{1,0:T(8,128)}), f32[432,3072]{1,0:T(8,128)}) %reduce-scatter.3.cloned.1.call-update) | async-done | bytes 5308432 | tf_op jit(solution)/shard_map/reduce_scatter | solution.py:83
  422.8 29.1 %all-reduce = (f32[1536,8]{0,1:T(8,128)S(1)}, f32[432]{0:T(512)S(1)}) all-reduce(f32[1536,8]{0,1:T(8,128)S(1)} %convolution_bitcast_fusion, f32[432]{0:T(512)S(1)} %multiply_reduce_fusion), channel_id=1, replica_groups=mesh['tok'=4,'hid'=8] {'hid'}, use_global_device_ids=true, to_apply=%region_2.3 | all-reduce | flops 12720 | bytes 101760 | tf_op jit(solution)/shard_map/psum | solution.py:70
  458.2 11.5 %reshape.153 = bf16[1536,2048,1]{1,0,2:T(8,128)(2,1)} reshape(bf16[1536,2,1024]{2,1,0:T(2,128)(2,1)} %param.10) | data formatting | bytes 12582912 | tf_op jit(solution)/shard_map/reshape | solution.py:76
  469.8 91.8 %all-gather.8.cloned.1.call-done = bf16[1728,3072]{1,0:T(8,128)(2,1)} async-done(((bf16[432,3072]{1,0:T(8,128)(2,1)}), bf16[1728,3072]{1,0:T(8,128)(2,1)}) %all-gather.8.cloned.1.call-update) | async-done | bytes 10616848 | tf_op jit(solution)/shard_map/all_gather | solution.py:99
  564.7 13.5 %fusion.28 = f32[4,432,1536]{2,1,0:T(8,128)S(1)} fusion(bf16[4,432,2048]{2,1,0:T(8,128)(2,1)S(1)} %bitcast.74, bf16[1536,2048,1]{1,0,2:T(8,128)(2,1)} %reshape.153), kind=kOutput, calls=%fused_computation.81 | convolution fusion | flops 10871635968 | bytes 23986176 | tf_op jit(solution)/shard_map/dot_general | solution.py:21
  578.2 119.8 %all_to_all.54 = f32[4,432,1536]{2,1,0:T(8,128)S(1)} all-to-all(f32[4,432,1536]{2,1,0:T(8,128)S(1)} %fusion.28), channel_id=1, replica_groups=mesh['tok'=4,'hid'=8] {'tok'}, dimensions={0} | all-to-all | bytes 21233664 | tf_op jit(solution)/shard_map/all_to_all | solution.py:118
  698.0 5.3 copy.34
  703.4 9.5 %gather_fusion.1 = f32[1536]{0:T(1024)S(1)} fusion(f32[432]{0:T(512)S(1)} %get-tuple-element.5, s32[2048]{0:T(1024)S(1)} %pad_clamp_fusion), kind=kCustom, calls=%fused_computation.1 | custom fusion | bytes 18432 | tf_op jit(solution)/shard_map/jit(_take)/gather | solution.py:125
  717.0 5.5 convolution_convert_fusion
  727.4 5.1 convolution_convert_fusion.1
  737.0 8.1 convolution_convert_fusion.2
  745.1 4.7 pad_maximum_fusion.2
  753.2 8.1 convolution_convert_fusion.3
  761.3 7.8 pad_maximum_fusion.1
  769.1 13.3 %convert_add_fusion = f32[1536,3072]{1,0:T(8,128)} fusion(bf16[1536,3072]{1,0:T(8,128)(2,1)S(1)} %pad_maximum_fusion.4, bf16[1536,3072]{1,0:T(8,128)(2,1)S(1)} %pad_maximum_fusion.3, bf16[1536,3072]{1,0:T(8,128)(2,1)S(1)} %pad_maximum_fusion.2, bf16[1536,3072]{1,0:T(8,128)(2,1)} %pad_maximum_fusion.1), kind=kLoop, calls=%fused_computation.3 | loop fusion | flops 33030144 | bytes 56623104 | tf_op jit(solution)/shard_map/add | solution.py:114
  782.4 11.5 %slice.129 = f32[1536,2048]{1,0:T(8,128)} slice(f32[1536,3072]{1,0:T(8,128)} %convert_add_fusion), slice={[0:1536], [0:2048]} | slice | bytes 25165824 | tf_op jit(solution)/shard_map/slice | solution.py:129
  793.8 6.7 slice.130
  800.5 16.9 %reshape.135 = f32[1536,2,1024]{2,1,0:T(2,128)} reshape(f32[1536,2048]{1,0:T(8,128)} %slice.129) | data formatting | bytes 25165824 | tf_op jit(solution)/shard_map/reshape | solution.py:129
  817.4 8.2 gather_fusion
  (65 shorter events, 40.6 us)
Async XLA Ops:
  7.2 151.7 %copy-start = (bf16[1536,1024]{1,0:T(8,128)(2,1)S(1)}, bf16[1536,1024]{1,0:T(8,128)(2,1)}, u32[]{:S(2)}) copy-start(bf16[1536,1024]{1,0:T(8,128)(2,1)} %param.11) | copy-start | bytes 9437188
  7.2 67.4 %all-gather.6.cloned.1.call-start = ((), (), s32[]{:S(2)}) async-start(), calls=%async_computation.6 | async-start | bytes 5971968 | tf_op jit(solution)/shard_map/all_gather | solution.py:65
  9.4 442.6 %copy-start.4 = (pred[1536]{0:T(1024)(128)(4,1)}, pred[1536]{0:T(1024)(128)(4,1)S(1)}, u32[]{:S(2)}) copy-start(pred[1536]{0:T(1024)(128)(4,1)S(1)} %get-tuple-element.18) | copy-start | bytes 4612
  15.2 116.9 %all-gather.4.cloned.1.call-start = ((), (), s32[]{:S(2)}) async-start(), calls=%async_computation.5 | async-start | bytes 5971968 | tf_op jit(solution)/shard_map/all_gather | solution.py:64
  80.0 65.2 %all-to-all-start.1 = ((bf16[432,4,1536]{2,0,1:T(8,128)(2,1)}), bf16[432,4,1536]{2,0,1:T(8,128)(2,1)}, u32[]{:S(2)}, u32[]{:S(2)}) async-start(bf16[432,4,1536]{2,0,1:T(8,128)(2,1)} %bitcast.71), calls=%async_computation.1 | async-start | bytes 10616832 | tf_op jit(solution)/shard_map/all_to_all | solution.py:79
  145.2 64.2 %all-to-all-start = ((bf16[432,4,1536]{2,0,1:T(8,128)(2,1)}), bf16[432,4,1536]{2,0,1:T(8,128)(2,1)}, u32[]{:S(2)}, u32[]{:S(2)}) async-start(bf16[432,4,1536]{2,0,1:T(8,128)(2,1)} %bitcast.70), calls=%async_computation | async-start | bytes 10616832 | tf_op jit(solution)/shard_map/all_to_all | solution.py:78
  150.2 269.5 %reduce-scatter.3.cloned.1.call-start = ((), (), s32[]{:S(2)}) async-start(), calls=%async_computation.7 | async-start | bytes 26542080 | tf_op jit(solution)/shard_map/reduce_scatter | solution.py:83
  209.4 15.1 %copy-start.2 = (f32[1728,1024]{1,0:T(8,128)S(1)}, f32[1728,1024]{1,0:T(8,128)}, u32[]{:S(2)}) copy-start(f32[1728,1024]{1,0:T(8,128)} %fusion.27) | copy-start | bytes 21233668
  231.9 1.7 copy-start.3
  231.9 329.7 %all-gather.8.cloned.1.call-start = ((), (), s32[]{:S(2)}) async-start(), calls=%async_computation.8 | async-start | bytes 13271040 | tf_op jit(solution)/shard_map/all_gather | solution.py:99
  458.2 359.3 %reduce-scatter.5.cloned.1.call-start = ((), (), s32[]{:S(2)}) async-start(), calls=%async_computation.9 | async-start | bytes 11943936 | tf_op jit(solution)/shard_map/reduce_scatter | solution.py:119
  561.6 3.1 slice-start.3
  703.4 9.5 %copy-start.6 = (s32[1536,2]{0,1:T(2,128)S(1)}, s32[1536,2]{0,1:T(2,128)}, u32[]{:S(2)}) copy-start(s32[1536,2]{0,1:T(2,128)} %param.8) | copy-start | bytes 36868
  717.0 6.4 slice-start
  717.0 6.4 slice-start.1
  722.6 1.6 slice-start.2
  817.4 8.2 copy-start.5
  817.4 8.2 copy-start.7
  817.4 11.7 %copy-start.1 = (bf16[1536,1024]{1,0:T(8,128)(2,1)S(1)}, bf16[1536,1024]{1,0:T(8,128)(2,1)}, u32[]{:S(2)}) copy-start(bf16[1536,1024]{1,0:T(8,128)(2,1)} %param.11) | copy-start | bytes 9437188
Sparse Core Ops, SparseCore 0:
  15.3 59.2 all-gather.5
  76.8 55.2 all-gather.3
  232.0 187.5 reduce-scatter.2
  458.3 103.2 all-gather.7
  703.5 110.0 reduce-scatter.4
where the time goes:
time: 841 us; the launch traced here: 836 us
  waiting for transfers between devices  431 us (51%)
  blocking collectives  149 us (18%)
  local copies, waits for them, and re-layouts  95.3 us (11%)
  matrix products  84.9 us (10%)
  other arithmetic  50.7 us (6%)
  between operations  14.6 us (2%)
  starting transfers between devices  11 us (1%)
    reduce_scatter x1, waiting for transfers between devices, local(): lax.psum_scatter(jnp.concatenate([jnp.dot(rows_in, weights_in, preferred_...  185 us
    all_to_all x1, blocking collectives, local(): lax.all_to_all(block, 'tok', split_axis=0, concat_axis=1, tiled=True)  120 us
    all_gather x1, waiting for transfers between devices, local(): piece = lax.all_gather(packed, 'tok', axis=0, tiled=True)  91.8 us
    all_gather x1, waiting for transfers between devices, local(): lax.all_gather(dispatched[:, local_cols:], 'hid', axis=1, tiled=True)  58.6 us
    all_gather x1, waiting for transfers between devices, local(): lax.all_gather(dispatched[:, :local_cols], 'hid', axis=1, tiled=True)  47 us
    all_to_all x1, waiting for transfers between devices, local(): lax.all_to_all(expert_in, 'tok', split_axis=1, concat_axis=0, tiled=True)  40.3 us
    dot_general x8, matrix products, contract_rows(): lax.dot_general(left, right, (((0,), (0,)), ((), ())), preferred_element_...  40.1 us
    psum x1, blocking collectives, local(): logits = lax.psum(contract_cols(tokens, router_cols), 'hid')  29.1 us
  transfers between devices with their start and end apart: 7, of which 6 were waited for; matrix products, arithmetic and copies ran while one was open for 19% of the time, Pallas kernels for 0%

commit v1 on v0

--- a/solution.py
+++ b/solution.py
@@ -96,7 +96,12 @@
         sums[:, : 2 * hidden_local], sums[:, 2 * hidden_local :], slot_gate
     )
     packed = jnp.concatenate([grads_mid, scaled], axis=1)
-    piece = lax.all_gather(packed, "tok", axis=0, tiled=True)
+    ring = [packed]
+    for hop in range(3):
+        ring.append(lax.ppermute(ring[-1], "tok", [(dev, (dev + 1) % 4) for dev in range(4)]))
+    piece = jnp.roll(
+        jnp.concatenate(ring[::-1], axis=0), (lax.axis_index("tok") + 1) * ring[0].shape[0], axis=0
+    )
     start = jnp.int32(0)
     grad_sum = jnp.zeros((weight_rows, 3 * hidden_local), jnp.float32)
     for group in range(piece.shape[0] // CAP):

time: 841 us -> 937 us (1.11)
  waiting for transfers between devices: 431 us -> 503 us
  local copies, waits for them, and re-layouts: 95.3 us -> 115 us
    ppermute x0 -> x3, waiting for transfers between devices: none -> 156 us  [local(): lax.ppermute(ring[-1], 'tok', [(dev, (dev + 1) % 4) for dev in range(4)])]
    all_gather x1 -> x0, waiting for transfers between devices: 91.8 us -> none  [local(): piece = lax.all_gather(packed, 'tok', axis=0, tiled=True)]
    unnamed x23 -> x33, local copies, waits for them, and re-layouts: 10.5 us -> 29 us
  transfers between devices with their start and end apart: 7 -> 9, of which waited for: 6 -> 9; matrix products, arithmetic and copies ran while one was open for 19% -> 17% of each run, Pallas kernels for 0% -> 0%
where the time goes in v1:
time: 937 us; the launch traced here: 928 us
  waiting for transfers between devices  503 us (54%)
  blocking collectives  143 us (15%)
  local copies, waits for them, and re-layouts  115 us (12%)
  matrix products  85.9 us (9%)
  other arithmetic  53 us (6%)
  between operations  14.3 us (2%)
  starting transfers between devices  13.7 us (1%)
    reduce_scatter x1, waiting for transfers between devices, local(): lax.psum_scatter(jnp.concatenate([jnp.dot(rows_in, weights_in, preferred_...  185 us
    ppermute x3, waiting for transfers between devices, local(): lax.ppermute(ring[-1], 'tok', [(dev, (dev + 1) % 4) for dev in range(4)])  156 us
    all_to_all x1, blocking collectives, local(): lax.all_to_all(block, 'tok', split_axis=0, concat_axis=1, tiled=True)  114 us
    all_gather x1, waiting for transfers between devices, local(): lax.all_gather(dispatched[:, local_cols:], 'hid', axis=1, tiled=True)  58.6 us
    all_gather x1, waiting for transfers between devices, local(): lax.all_gather(dispatched[:, :local_cols], 'hid', axis=1, tiled=True)  47 us
    dot_general x8, matrix products, contract_rows(): lax.dot_general(left, right, (((0,), (0,)), ((), ())), preferred_element_...  41.2 us
    all_to_all x1, waiting for transfers between devices, local(): lax.all_to_all(expert_in, 'tok', split_axis=1, concat_axis=0, tiled=True)  40.7 us
    psum x1, blocking collectives, local(): logits = lax.psum(contract_cols(tokens, router_cols), 'hid')  29.1 us
  transfers between devices with their start and end apart: 9, of which 9 were waited for; matrix products, arithmetic and copies ran while one was open for 17% of the time, Pallas kernels for 0%

profile of v1, /device:TPU:0, one launch (start us, length us, event | category | flops | bytes accessed | tf_op | source)
XLA Modules:
  0.0 928.3 jit_solution(11078693574408264709)
XLA Ops:
  16.6 58.6 %all-gather.5.cloned.1.call-done = bf16[432,6144]{1,0:T(8,128)(2,1)} async-done(((bf16[432,768]{1,0:T(8,128)(2,1)}), bf16[432,6144]{1,0:T(8,128)(2,1)}) %all-gather.5.cloned.1.call-update) | async-done | bytes 5308432 | tf_op jit(solution)/shard_map/all_gather | solution.py:65
  75.2 5.3 copy.41
  85.7 47.0 %all-gather.3.cloned.1.call-done = bf16[432,6144]{1,0:T(8,128)(2,1)} async-done(((bf16[432,768]{1,0:T(8,128)(2,1)}), bf16[432,6144]{1,0:T(8,128)(2,1)}) %all-gather.3.cloned.1.call-update) | async-done | bytes 5308432 | tf_op jit(solution)/shard_map/all_gather | solution.py:64
  132.7 5.4 copy.42
  138.1 7.7 all-to-all-done.1
  151.1 8.1 copy.36
  159.2 10.2 %fusion.31 = f32[1728,1024]{1,0:T(8,128)} fusion(bf16[1728,1536]{1,0:T(8,128)(2,1)} %bitcast.5, bf16[1536,1024]{1,0:T(8,128)(2,1)S(1)} %copy-done), kind=kOutput, calls=%fused_computation.93 | convolution fusion | flops 5435817984 | bytes 15532032 | tf_op jit(solution)/shard_map/dot_general | solution.py:87
  169.3 40.7 %all-to-all-done = bf16[432,4,1536]{2,0,1:T(8,128)(2,1)} async-done(((bf16[432,4,1536]{2,0,1:T(8,128)(2,1)}), bf16[432,4,1536]{2,0,1:T(8,128)(2,1)}, u32[]{:S(2)}, u32[]{:S(2)}) %all-to-all-start) | async-done | bytes 5308448 | tf_op jit(solution)/shard_map/all_to_all | solution.py:78
  210.0 15.1 %fusion.30 = f32[1728,2048]{1,0:T(8,128)S(1)} fusion(bf16[1728,1536]{1,0:T(8,128)(2,1)} %bitcast.3, bf16[1536,2048]{1,0:T(8,128)(2,1)} %bitcast.73), kind=kOutput, calls=%fused_computation.92 | convolution fusion | flops 10871635968 | bytes 25755648 | tf_op jit(solution)/shard_map/dot_general | solution.py:86
  225.1 7.5 pad_maximum_fusion
  235.7 184.7 %reduce-scatter.3.cloned.1.call-done = f32[432,3072]{1,0:T(8,128)} async-done(((f32[1728,3072]{1,0:T(8,128)}), f32[432,3072]{1,0:T(8,128)}) %reduce-scatter.3.cloned.1.call-update) | async-done | bytes 5308432 | tf_op jit(solution)/shard_map/reduce_scatter | solution.py:83
  423.5 29.1 %all-reduce = (f32[1536,8]{0,1:T(8,128)S(1)}, f32[432]{0:T(512)S(1)}) all-reduce(f32[1536,8]{0,1:T(8,128)S(1)} %convolution_bitcast_fusion, f32[432]{0:T(512)S(1)} %multiply_reduce_fusion), channel_id=1, replica_groups=mesh['tok'=4,'hid'=8] {'hid'}, use_global_device_ids=true, to_apply=%region_2.3 | all-reduce | flops 12720 | bytes 101760 | tf_op jit(solution)/shard_map/psum | solution.py:70
  458.9 55.3 %collective-permute-done = bf16[432,3072]{1,0:T(8,128)(2,1)S(1)} collective-permute-done((bf16[432,3072]{1,0:T(8,128)(2,1)S(1)}, bf16[432,3072]{1,0:T(8,128)(2,1)S(1)}, u32[]{:S(2)}, u32[]{:S(2)}) %collective-permute-start) | collective-permute-done | bytes 2654240 | tf_op jit(solution)/shard_map/ppermute | solution.py:101
  516.7 56.6 %collective-permute-done.1 = bf16[432,3072]{1,0:T(8,128)(2,1)} collective-permute-done((bf16[432,3072]{1,0:T(8,128)(2,1)S(1)}, bf16[432,3072]{1,0:T(8,128)(2,1)}, u32[]{:S(2)}, u32[]{:S(2)}) %collective-permute-start.1) | collective-permute-done | bytes 2654240 | tf_op jit(solution)/shard_map/ppermute | solution.py:101
  573.9 11.1 %reshape.153 = bf16[1536,2048,1]{1,0,2:T(8,128)(2,1)} reshape(bf16[1536,2,1024]{2,1,0:T(2,128)(2,1)} %param.10) | data formatting | bytes 12582912 | tf_op jit(solution)/shard_map/reshape | solution.py:76
  585.0 43.7 %collective-permute-done.2 = bf16[432,3072]{1,0:T(8,128)(2,1)} collective-permute-done((bf16[432,3072]{1,0:T(8,128)(2,1)}, bf16[432,3072]{1,0:T(8,128)(2,1)}, u32[]{:S(2)}, u32[]{:S(2)}) %collective-permute-start.2) | collective-permute-done | bytes 2654240 | tf_op jit(solution)/shard_map/ppermute | solution.py:101
  649.2 5.2 constant_dynamic-slice_fusion
  654.4 13.5 %fusion.32 = f32[4,432,1536]{2,1,0:T(8,128)S(1)} fusion(bf16[4,432,2048]{2,1,0:T(8,128)(2,1)S(1)} %bitcast.72, bf16[1536,2048,1]{1,0,2:T(8,128)(2,1)} %reshape.153), kind=kOutput, calls=%fused_computation.94 | convolution fusion | flops 10871635968 | bytes 23986176 | tf_op jit(solution)/shard_map/dot_general | solution.py:21
  667.9 114.2 %all_to_all.54 = f32[4,432,1536]{2,1,0:T(8,128)S(1)} all-to-all(f32[4,432,1536]{2,1,0:T(8,128)S(1)} %fusion.32), channel_id=1, replica_groups=mesh['tok'=4,'hid'=8] {'tok'}, dimensions={0} | all-to-all | bytes 21233664 | tf_op jit(solution)/shard_map/all_to_all | solution.py:123
  782.1 5.4 copy.34
  788.2 9.5 %gather_fusion.1 = f32[1536]{0:T(1024)S(1)} fusion(f32[432]{0:T(512)S(1)} %get-tuple-element.5, s32[2048]{0:T(1024)S(1)} %pad_clamp_fusion), kind=kCustom, calls=%fused_computation.1 | custom fusion | bytes 18432 | tf_op jit(solution)/shard_map/jit(_take)/gather | solution.py:130
  801.9 5.4 convolution_convert_fusion
  811.8 5.4 convolution_convert_fusion.1
  821.6 8.1 convolution_convert_fusion.2
  838.2 8.1 convolution_convert_fusion.3
  846.4 7.8 pad_maximum_fusion.1
  854.1 13.0 %convert_add_fusion = f32[1536,3072]{1,0:T(8,128)} fusion(bf16[1536,3072]{1,0:T(8,128)(2,1)S(1)} %pad_maximum_fusion.4, bf16[1536,3072]{1,0:T(8,128)(2,1)S(1)} %pad_maximum_fusion.3, bf16[1536,3072]{1,0:T(8,128)(2,1)S(1)} %pad_maximum_fusion.2, bf16[1536,3072]{1,0:T(8,128)(2,1)} %pad_maximum_fusion.1), kind=kLoop, calls=%fused_computation.3 | loop fusion | flops 33030144 | bytes 56623104 | tf_op jit(solution)/shard_map/add | solution.py:119
  867.1 11.5 %slice.120 = f32[1536,2048]{1,0:T(8,128)} slice(f32[1536,3072]{1,0:T(8,128)} %convert_add_fusion), slice={[0:1536], [0:2048]} | slice | bytes 25165824 | tf_op jit(solution)/shard_map/slice | solution.py:134
  878.6 6.6 slice.121
  885.2 16.9 %reshape.135 = f32[1536,2,1024]{2,1,0:T(2,128)} reshape(f32[1536,2048]{1,0:T(8,128)} %slice.120) | data formatting | bytes 25165824 | tf_op jit(solution)/shard_map/reshape | solution.py:134
  902.1 7.8 reduce-scatter.5.cloned.1.call-done
  909.9 8.2 gather_fusion
  (78 shorter events, 81.6 us)
Async XLA Ops:
  7.2 152.0 %copy-start = (bf16[1536,1024]{1,0:T(8,128)(2,1)S(1)}, bf16[1536,1024]{1,0:T(8,128)(2,1)}, u32[]{:S(2)}) copy-start(bf16[1536,1024]{1,0:T(8,128)(2,1)} %param.11) | copy-start | bytes 9437188
  7.2 68.0 %all-gather.5.cloned.1.call-start = ((), (), s32[]{:S(2)}) async-start(), calls=%async_computation.6 | async-start | bytes 5971968 | tf_op jit(solution)/shard_map/all_gather | solution.py:65
  8.1 6.5 copy-start.7
  10.0 442.8 %copy-start.9 = (pred[1536]{0:T(1024)(128)(4,1)}, pred[1536]{0:T(1024)(128)(4,1)S(1)}, u32[]{:S(2)}) copy-start(pred[1536]{0:T(1024)(128)(4,1)S(1)} %get-tuple-element.18) | copy-start | bytes 4612
  15.8 116.9 %all-gather.3.cloned.1.call-start = ((), (), s32[]{:S(2)}) async-start(), calls=%async_computation.5 | async-start | bytes 5971968 | tf_op jit(solution)/shard_map/all_gather | solution.py:64
  80.6 65.2 %all-to-all-start.1 = ((bf16[432,4,1536]{2,0,1:T(8,128)(2,1)}), bf16[432,4,1536]{2,0,1:T(8,128)(2,1)}, u32[]{:S(2)}, u32[]{:S(2)}) async-start(bf16[432,4,1536]{2,0,1:T(8,128)(2,1)} %bitcast.71), calls=%async_computation.1 | async-start | bytes 10616832 | tf_op jit(solution)/shard_map/all_to_all | solution.py:79
  145.7 64.3 %all-to-all-start = ((bf16[432,4,1536]{2,0,1:T(8,128)(2,1)}), bf16[432,4,1536]{2,0,1:T(8,128)(2,1)}, u32[]{:S(2)}, u32[]{:S(2)}) async-start(bf16[432,4,1536]{2,0,1:T(8,128)(2,1)} %bitcast.70), calls=%async_computation | async-start | bytes 10616832 | tf_op jit(solution)/shard_map/all_to_all | solution.py:78
  150.8 269.6 %reduce-scatter.3.cloned.1.call-start = ((), (), s32[]{:S(2)}) async-start(), calls=%async_computation.7 | async-start | bytes 26542080 | tf_op jit(solution)/shard_map/reduce_scatter | solution.py:83
  210.0 15.1 %copy-start.4 = (f32[1728,1024]{1,0:T(8,128)S(1)}, f32[1728,1024]{1,0:T(8,128)}, u32[]{:S(2)}) copy-start(f32[1728,1024]{1,0:T(8,128)} %fusion.31) | copy-start | bytes 21233668
  232.6 1.7 copy-start.5
  232.7 677.2 %reduce-scatter.5.cloned.1.call-start = ((), (), s32[]{:S(2)}) async-start(), calls=%async_computation.8 | async-start | bytes 11943936 | tf_op jit(solution)/shard_map/reduce_scatter | solution.py:124
  457.4 56.9 %collective-permute-start = (bf16[432,3072]{1,0:T(8,128)(2,1)S(1)}, bf16[432,3072]{1,0:T(8,128)(2,1)S(1)}, u32[]{:S(2)}, u32[]{:S(2)}) collective-permute-start(bf16[432,3072]{1,0:T(8,128)(2,1)S(1)} %pad_maximum_fusion.5), channel_id=1, source_target_pairs={{0,8},{8,16},{16,24},{24,0},{1,9},{9,17},{17,25},{25,1},{2,10},{10... | collective-permute-start | bytes 7962632 | tf_op jit(solution)/shard_map/ppermute | solution.py:101
  514.3 1.5 copy-start.2
  515.8 57.5 %collective-permute-start.1 = (bf16[432,3072]{1,0:T(8,128)(2,1)S(1)}, bf16[432,3072]{1,0:T(8,128)(2,1)}, u32[]{:S(2)}, u32[]{:S(2)}) collective-permute-start(bf16[432,3072]{1,0:T(8,128)(2,1)S(1)} %collective-permute-done), channel_id=1, source_target_pairs={{0,8},{8,16},{16,24},{24,0},{1,9},{9,17},{17,25},{25,1},{2,10},{10... | collective-permute-start | bytes 7962632 | tf_op jit(solution)/shard_map/ppermute | solution.py:101
  573.3 55.4 %collective-permute-start.2 = (bf16[432,3072]{1,0:T(8,128)(2,1)}, bf16[432,3072]{1,0:T(8,128)(2,1)}, u32[]{:S(2)}, u32[]{:S(2)}) collective-permute-start(bf16[432,3072]{1,0:T(8,128)(2,1)} %collective-permute-done.1), channel_id=1, source_target_pairs={{0,8},{8,16},{16,24},{24,0},{1,9},{9,17},{17,25},{25,1},{2,10},{10... | collective-permute-start | bytes 7962632 | tf_op jit(solution)/shard_map/ppermute | solution.py:101
  585.0 50.5 %copy-start.3 = (bf16[432,3072]{1,0:T(8,128)(2,1)S(1)}, bf16[432,3072]{1,0:T(8,128)(2,1)}, u32[]{:S(2)}) copy-start(bf16[432,3072]{1,0:T(8,128)(2,1)} %copy-done.2) | copy-start | bytes 7962628
  787.5 0.7 copy-start.6
  787.5 10.2 %copy-start.8 = (pred[1536,1]{0,1:T(4,128)(4,1)S(1)}, pred[1536,1]{0,1:T(4,128)(4,1)}, u32[]{:S(2)}) copy-start(pred[1536,1]{0,1:T(4,128)(4,1)} %copy-done.7) | copy-start | bytes 4612
  787.5 10.2 %copy-start.11 = (s32[1536,2]{0,1:T(2,128)S(1)}, s32[1536,2]{0,1:T(2,128)}, u32[]{:S(2)}) copy-start(s32[1536,2]{0,1:T(2,128)} %param.8) | copy-start | bytes 36868
  902.1 15.9 %copy-start.10 = (pred[1536]{0:T(1024)(128)(4,1)S(1)}, pred[1536]{0:T(1024)(128)(4,1)}, u32[]{:S(2)}) copy-start(pred[1536]{0:T(1024)(128)(4,1)} %copy-done.9) | copy-start | bytes 4612
  902.1 15.9 %copy-start.12 = (pred[1536]{0:T(1024)(128)(4,1)S(1)}, pred[1536]{0:T(1024)(128)(4,1)}, u32[]{:S(2)}) copy-start(pred[1536]{0:T(1024)(128)(4,1)} %get-tuple-element.8) | copy-start | bytes 4612
  909.9 11.7 %copy-start.1 = (bf16[1536,1024]{1,0:T(8,128)(2,1)S(1)}, bf16[1536,1024]{1,0:T(8,128)(2,1)}, u32[]{:S(2)}) copy-start(bf16[1536,1024]{1,0:T(8,128)(2,1)} %param.11) | copy-start | bytes 9437188
Sparse Core Ops, SparseCore 0:
  15.9 59.2 all-gather.4
  77.4 55.2 all-gather.2
  232.8 187.5 reduce-scatter.2
  787.6 122.2 reduce-scatter.4
